TPU v7x, 32 devices: a whole 2x2x4 slice. The times are simulated.
32 devices in a mesh: dp: 8 (over z, x), mp: 4 (over y, core).
Axes of the slice: x: 2, y: 2, z: 4, core: 2. Of those that a mesh axis runs over, the one named last changes fastest.
Arguments:
- patches: bfloat16 [8, 2048, 768], P('dp'), may hold values from -6 to 6
- cotangent: bfloat16 [8, 2048, 768], P('dp'), may hold values from -6 to 6
- keep_mask: int32 [8, 2048], P('dp'), may hold values from 0 to 1, as said below
- segment_ids: int32 [8, 2048], P('dp'), may hold values from 0 to 7, never falling along the last dimension, each value on 1 to 512 neighbouring positions
- step_count: int32 [1], replicated, may hold values from 2 to 8
- qkv_weight: float32 [3, 768, 768], P(None, None, 'mp'), may hold values from -0.21875 to 0.21875
- qkv_first: float32 [3, 768, 768], P(None, 'dp', 'mp'), may hold values from -0.00061035156 to 0.00061035156
- qkv_second: float32 [3, 768, 768], P(None, 'dp', 'mp'), may hold values from 7.4315953e-09 to 2.9669868e-08
- out_weight: float32 [768, 768], P('mp'), may hold values from -1.75 to 1.75
- out_first: float32 [768, 768], P('mp', 'dp'), may hold values from -0.00061035156 to 0.00061035156
- out_second: float32 [768, 768], P('mp', 'dp'), may hold values from 7.4315953e-09 to 2.9669868e-08
- up_weight: float32 [768, 3072], P(None, 'mp'), may hold values from -0.21875 to 0.21875
- up_first: float32 [768, 3072], P('dp', 'mp'), may hold values from -0.00061035156 to 0.00061035156
- up_second: float32 [768, 3072], P('dp', 'mp'), may hold values from 7.4315953e-09 to 2.9669868e-08
- down_weight: float32 [3072, 768], P('mp'), may hold values from -0.109375 to 0.109375
- down_first: float32 [3072, 768], P('mp', 'dp'), may hold values from -0.00061035156 to 0.00061035156
- down_second: float32 [3072, 768], P('mp', 'dp'), may hold values from 7.4315953e-09 to 2.9669868e-08
- head_params: float32 [5, 12, 64], P(None, 'mp'), may hold values from -2 to 2, as said below
- head_first: float32 [5, 12, 64], P(None, 'mp'), may hold values from -0.00061035156 to 0.00061035156
- head_second: float32 [5, 12, 64], P(None, 'mp'), may hold values from 7.4315953e-09 to 2.9669868e-08
- up_bias: float32 [3072], P('mp'), may hold values from -2 to 2
- upb_first: float32 [3072], P('mp'), may hold values from -0.00061035156 to 0.00061035156
- upb_second: float32 [3072], P('mp'), may hold values from 7.4315953e-09 to 2.9669868e-08
- vec_params: float32 [6, 768], replicated, may hold values from -2 to 2, as said below
- vec_first: float32 [6, 768], replicated, may hold values from -0.00061035156 to 0.00061035156
- vec_second: float32 [6, 768], replicated, may hold values from 7.4315953e-09 to 2.9669868e-08
Outputs:
- block_out: bfloat16 [8, 2048, 768], P('dp')
- grad_input: bfloat16 [8, 2048, 768], P('dp')
- new_qkv: float32 [3, 768, 768], P(None, 'dp', 'mp')
- new_qkv_first: float32 [3, 768, 768], P(None, 'dp', 'mp')
- new_qkv_second: float32 [3, 768, 768], P(None, 'dp', 'mp')
- new_out: float32 [768, 768], P('mp', 'dp')
- new_out_first: float32 [768, 768], P('mp', 'dp')
- new_out_second: float32 [768, 768], P('mp', 'dp')
- new_up: float32 [768, 3072], P('dp', 'mp')
- new_up_first: float32 [768, 3072], P('dp', 'mp')
- new_up_second: float32 [768, 3072], P('dp', 'mp')
- new_down: float32 [3072, 768], P('mp', 'dp')
- new_down_first: float32 [3072, 768], P('mp', 'dp')
- new_down_second: float32 [3072, 768], P('mp', 'dp')
- new_head: float32 [5, 12, 64], P(None, 'mp')
- new_head_first: float32 [5, 12, 64], P(None, 'mp')
- new_head_second: float32 [5, 12, 64], P(None, 'mp')
- new_upb: float32 [3072], P('mp')
- new_upb_first: float32 [3072], P('mp')
- new_upb_second: float32 [3072], P('mp')
- new_vec: float32 [6, 768], replicated
- new_vec_first: float32 [6, 768], replicated
- new_vec_second: float32 [6, 768], replicated
- grad_norm: float32 [1], replicated
- rms_stats: float32 [2], replicated
Inputs may be any that keep to these rules, and one draw needn't show every extreme that they name: `keep_mask`: per sequence each patch is kept with a chance from one half to all; the chance rises with the sequence index. `segment_ids`: within a row ids never fall; each image covers 1 to 512 consecutive slots, one exactly that many. `head_params`: rows 0 to 2 are biases, rows 3 and 4 gains. `vec_params`: rows 0 and 2 are gains, the others biases.
All inputs are finite; a program needn't handle non-finite values.
Results may differ from a plain program's by a relative error of at most 0.012.
Values sent between devices are 32-bit elements; how exact they have to be, the bound alone decides.
No kernel may reach another device: no remote copies, remote signals or barrier semaphores. Data moves between devices by JAX's collectives and lax.ppermute only.
A program may use at most 256 MiB of HBM per device.

v0:
```python
import jax
import jax.numpy as jnp
from jax import lax
from jax.sharding import PartitionSpec as P

NORM_EPS = 1e-06
CLIP_LIMIT = 1.0
LEARN_RATE = 0.1
BETA_ONE = 0.9
BETA_TWO = 0.95
ADAM_EPS = 1e-08
WEIGHT_DECAY = 0.1


def standardize(values):
    center = values - jnp.mean(values, axis=-1, keepdims=True)
    spread = jnp.mean(center * center, axis=-1, keepdims=True)
    factor = lax.rsqrt(spread + NORM_EPS)
    return (center * factor, factor)


def norm_back(grad_hat, normed, factor):
    return factor * (
        grad_hat
        - jnp.mean(grad_hat, axis=-1, keepdims=True)
        - normed * jnp.mean(grad_hat * normed, axis=-1, keepdims=True)
    )


def adam_step(weight, grad, first, second, factor, corr_one, corr_two, decay):
    grad = factor * grad
    first = BETA_ONE * first + (1.0 - BETA_ONE) * grad
    second = BETA_TWO * second + (1.0 - BETA_TWO) * grad * grad
    update = first / corr_one / (jnp.sqrt(second / corr_two) + ADAM_EPS)
    return (weight - LEARN_RATE * (update + decay * weight), first, second)


def local(
    patches,
    cotangent,
    keep_mask,
    segment_ids,
    step_count,
    qkv_weight,
    qkv_first,
    qkv_second,
    out_weight,
    out_first,
    out_second,
    up_weight,
    up_first,
    up_second,
    down_weight,
    down_first,
    down_second,
    head_params,
    head_first,
    head_second,
    up_bias,
    upb_first,
    upb_second,
    vec_params,
    vec_first,
    vec_second,
):
    seq_len = patches.shape[1]
    width = patches.shape[2]
    heads_here = head_params.shape[1]
    head_dim = head_params.shape[2]
    local_width = heads_here * head_dim
    head_scale = head_dim ** (-0.5)
    inputs = patches[0].astype(jnp.float32)
    keep_row = keep_mask[0]
    seg_row = segment_ids[0]
    keep_f = keep_row.astype(jnp.float32)
    places = jnp.arange(seq_len)
    xh_first, rs_first = standardize(inputs)
    a_first = (xh_first * vec_params[0] + vec_params[1]).astype(jnp.bfloat16)
    qkv_low = qkv_weight.astype(jnp.bfloat16)
    raw = jnp.einsum("sd,kde->kse", a_first, qkv_low, preferred_element_type=jnp.float32)
    raw = raw + head_params[0:3].reshape(3, 1, local_width)
    query = raw[0].reshape(seq_len, heads_here, head_dim)
    key_raw = raw[1].reshape(seq_len, heads_here, head_dim)
    value = raw[2].reshape(seq_len, heads_here, head_dim)
    q_hat, q_factor = standardize(query)
    k_hat, k_factor = standardize(key_raw)
    q_in = (q_hat * head_params[3] * head_scale).astype(jnp.bfloat16)
    k_in = (k_hat * head_params[4]).astype(jnp.bfloat16)
    v_in = value.astype(jnp.bfloat16)
    block = min(512, seq_len)
    blocks = seq_len // block

    def block_scores(start):
        q_block = q_in[start : start + block]
        scores = jnp.einsum("qhd,khd->hqk", q_block, k_in, preferred_element_type=jnp.float32)
        allowed = (seg_row[start : start + block, None] == seg_row[None, :]) & (
            (keep_row[None, :] == 1) | (places[start : start + block, None] == places[None, :])
        )
        return (jnp.where(allowed[None], scores, -1e30), q_block)

    outs_list = []
    lse_list = []
    for index in range(blocks):
        scores, q_block = block_scores(index * block)
        top = jnp.max(scores, axis=-1, keepdims=True)
        expo = jnp.exp(scores - top)
        total = jnp.sum(expo, axis=-1, keepdims=True)
        probs = (expo / total).astype(jnp.bfloat16)
        lse_list.append(top + jnp.log(total))
        outs_list.append(
            jnp.einsum("hqk,khd->qhd", probs, v_in, preferred_element_type=jnp.float32)
        )
    mixed = jnp.concatenate(outs_list, axis=0).reshape(seq_len, local_width).astype(jnp.bfloat16)
    out_low = out_weight.astype(jnp.bfloat16)
    attn = (
        lax.psum(jnp.dot(mixed, out_low, preferred_element_type=jnp.float32), "mp") + vec_params[4]
    )
    hidden = inputs + attn
    xh_second, rs_second = standardize(hidden)
    a_second = (xh_second * vec_params[2] + vec_params[3]).astype(jnp.bfloat16)
    up_low = up_weight.astype(jnp.bfloat16)
    upper = jnp.dot(a_second, up_low, preferred_element_type=jnp.float32) + up_bias
    gelu_value, gelu_back = jax.vjp(lambda val: jax.nn.gelu(val, approximate=False), upper)
    gated = gelu_value.astype(jnp.bfloat16)
    down_low = down_weight.astype(jnp.bfloat16)
    mlp = (
        lax.psum(jnp.dot(gated, down_low, preferred_element_type=jnp.float32), "mp") + vec_params[5]
    )
    result = hidden + mlp
    count_here = jnp.sum(keep_f)
    attn_sq = jnp.sum(keep_f[:, None] * attn * attn)
    mlp_sq = jnp.sum(keep_f[:, None] * mlp * mlp)
    count, attn_total, mlp_total = lax.psum((count_here, attn_sq, mlp_sq), "dp")
    grad_out = cotangent[0].astype(jnp.float32) * keep_f[:, None]
    grad_mlp = grad_out.astype(jnp.bfloat16)
    grad_bdown = jnp.sum(grad_mlp.astype(jnp.float32), axis=0)
    grad_down = jnp.einsum("sf,sd->fd", gated, grad_mlp, preferred_element_type=jnp.float32)
    grad_gated = jnp.einsum("sd,fd->sf", grad_mlp, down_low, preferred_element_type=jnp.float32)
    grad_upper = gelu_back(grad_gated)[0].astype(jnp.bfloat16)
    grad_bup = jnp.sum(grad_upper.astype(jnp.float32), axis=0)
    grad_up = jnp.einsum("sd,sf->df", a_second, grad_upper, preferred_element_type=jnp.float32)
    grad_xn2 = lax.psum(
        jnp.einsum("sf,df->sd", grad_upper, up_low, preferred_element_type=jnp.float32), "mp"
    )
    grad_gain2 = jnp.sum(grad_xn2 * xh_second, axis=0)
    grad_bias2 = jnp.sum(grad_xn2, axis=0)
    grad_hidden = grad_out + norm_back(grad_xn2 * vec_params[2], xh_second, rs_second)
    grad_attn = grad_hidden.astype(jnp.bfloat16)
    grad_bout = jnp.sum(grad_attn.astype(jnp.float32), axis=0)
    grad_outw = jnp.einsum("se,sd->ed", mixed, grad_attn, preferred_element_type=jnp.float32)
    grad_mixed = jnp.einsum("sd,ed->se", grad_attn, out_low, preferred_element_type=jnp.float32)
    grad_mixed = grad_mixed.astype(jnp.bfloat16).reshape(seq_len, heads_here, head_dim)
    grad_kin = jnp.zeros((seq_len, heads_here, head_dim), jnp.float32)
    grad_vin = jnp.zeros((seq_len, heads_here, head_dim), jnp.float32)
    grad_qlist = []
    for index in range(blocks):
        start = index * block
        scores, q_block = block_scores(start)
        probs_full = jnp.exp(scores - lse_list[index])
        probs = probs_full.astype(jnp.bfloat16)
        grad_block = grad_mixed[start : start + block]
        grad_vin = grad_vin + jnp.einsum(
            "hqk,qhd->khd", probs, grad_block, preferred_element_type=jnp.float32
        )
        grad_probs = jnp.einsum(
            "qhd,khd->hqk", grad_block, v_in, preferred_element_type=jnp.float32
        )
        delta = jnp.sum(probs_full * grad_probs, axis=-1, keepdims=True)
        grad_scores = (probs_full * (grad_probs - delta)).astype(jnp.bfloat16)
        grad_qlist.append(
            jnp.einsum("hqk,khd->qhd", grad_scores, k_in, preferred_element_type=jnp.float32)
        )
        grad_kin = grad_kin + jnp.einsum(
            "hqk,qhd->khd", grad_scores, q_block, preferred_element_type=jnp.float32
        )
    grad_qin = jnp.concatenate(grad_qlist, axis=0) * head_scale
    grad_qgain = jnp.sum(grad_qin * q_hat, axis=0)
    grad_query = norm_back(grad_qin * head_params[3], q_hat, q_factor)
    grad_kgain = jnp.sum(grad_kin * k_hat, axis=0)
    grad_key = norm_back(grad_kin * head_params[4], k_hat, k_factor)
    grad_raw = jnp.stack(
        [
            grad_query.reshape(seq_len, local_width),
            grad_key.reshape(seq_len, local_width),
            grad_vin.reshape(seq_len, local_width),
        ]
    ).astype(jnp.bfloat16)
    grad_bqkv = jnp.sum(grad_raw.astype(jnp.float32), axis=1)
    grad_qkv = jnp.einsum("sd,kse->kde", a_first, grad_raw, preferred_element_type=jnp.float32)
    grad_xn1 = lax.psum(
        jnp.einsum("kse,kde->sd", grad_raw, qkv_low, preferred_element_type=jnp.float32), "mp"
    )
    grad_gain1 = jnp.sum(grad_xn1 * xh_first, axis=0)
    grad_bias1 = jnp.sum(grad_xn1, axis=0)
    grad_inputs = grad_hidden + norm_back(grad_xn1 * vec_params[0], xh_first, rs_first)
    vec_grad = jnp.stack([grad_gain1, grad_bias1, grad_gain2, grad_bias2, grad_bout, grad_bdown])
    head_grad = jnp.concatenate(
        [grad_bqkv.reshape(3, heads_here, head_dim), jnp.stack([grad_qgain, grad_kgain])], axis=0
    )
    vec_grad, head_grad, bup_grad = lax.psum((vec_grad, head_grad, grad_bup), "dp")
    dp_rank = lax.axis_index("dp")
    rows = width // lax.axis_size("dp")
    start_row = dp_rank * rows
    summed = lax.psum((grad_qkv, grad_outw, grad_up, grad_down), "dp")
    shares = (
        lax.dynamic_slice_in_dim(summed[0], start_row, rows, 1),
        lax.dynamic_slice_in_dim(summed[1], start_row, rows, 1),
        lax.dynamic_slice_in_dim(summed[2], start_row, rows, 0),
        lax.dynamic_slice_in_dim(summed[3], start_row, rows, 1),
    )
    old_shares = (
        lax.dynamic_slice_in_dim(qkv_weight, start_row, rows, 1),
        lax.dynamic_slice_in_dim(out_weight, start_row, rows, 1),
        lax.dynamic_slice_in_dim(up_weight, start_row, rows, 0),
        lax.dynamic_slice_in_dim(down_weight, start_row, rows, 1),
    )
    first_dp = dp_rank == 0
    first_mp = lax.axis_index("mp") == 0
    big_sq = sum((jnp.sum(share * share) for share in shares))
    split_sq = jnp.sum(head_grad * head_grad) + jnp.sum(bup_grad * bup_grad)
    whole_sq = jnp.sum(vec_grad * vec_grad)
    raw_sq = (
        big_sq + jnp.where(first_dp, split_sq, 0.0) + jnp.where(first_dp & first_mp, whole_sq, 0.0)
    )
    sq_total = lax.psum(raw_sq, ("dp", "mp"))
    scale = seq_len * lax.axis_size("dp") / count
    grad_norm = scale * jnp.sqrt(sq_total)
    factor = jnp.minimum(1.0, CLIP_LIMIT / (grad_norm + 1e-06)) * scale
    steps_f = step_count[0].astype(jnp.float32)
    corr_one = 1.0 - BETA_ONE**steps_f
    corr_two = 1.0 - BETA_TWO**steps_f
    new_qkv = adam_step(
        old_shares[0], shares[0], qkv_first, qkv_second, factor, corr_one, corr_two, WEIGHT_DECAY
    )
    new_out = adam_step(
        old_shares[1], shares[1], out_first, out_second, factor, corr_one, corr_two, WEIGHT_DECAY
    )
    new_up = adam_step(
        old_shares[2], shares[2], up_first, up_second, factor, corr_one, corr_two, WEIGHT_DECAY
    )
    new_down = adam_step(
        old_shares[3], shares[3], down_first, down_second, factor, corr_one, corr_two, WEIGHT_DECAY
    )
    new_head = adam_step(
        head_params, head_grad, head_first, head_second, factor, corr_one, corr_two, 0.0
    )
    new_upb = adam_step(up_bias, bup_grad, upb_first, upb_second, factor, corr_one, corr_two, 0.0)
    new_vec = adam_step(
        vec_params, vec_grad, vec_first, vec_second, factor, corr_one, corr_two, 0.0
    )
    rms = jnp.sqrt(jnp.stack([attn_total, mlp_total]) / (count * width))
    return (
        result.astype(jnp.bfloat16)[None],
        (grad_inputs * scale).astype(jnp.bfloat16)[None],
        new_qkv[0],
        new_qkv[1],
        new_qkv[2],
        new_out[0],
        new_out[1],
        new_out[2],
        new_up[0],
        new_up[1],
        new_up[2],
        new_down[0],
        new_down[1],
        new_down[2],
        new_head[0],
        new_head[1],
        new_head[2],
        new_upb[0],
        new_upb[1],
        new_upb[2],
        new_vec[0],
        new_vec[1],
        new_vec[2],
        grad_norm.reshape(1),
        rms,
    )


def solution(mesh):
    placed = (
        P("dp", None, None),
        P("dp", None, None),
        P("dp", None),
        P("dp", None),
        P(),
        P(None, None, "mp"),
        P(None, "dp", "mp"),
        P(None, "dp", "mp"),
        P("mp", None),
        P("mp", "dp"),
        P("mp", "dp"),
        P(None, "mp"),
        P("dp", "mp"),
        P("dp", "mp"),
        P("mp", None),
        P("mp", "dp"),
        P("mp", "dp"),
        P(None, "mp", None),
        P(None, "mp", None),
        P(None, "mp", None),
        P("mp"),
        P("mp"),
        P("mp"),
        P(),
        P(),
        P(),
    )
    return jax.shard_map(
        local,
        mesh=mesh,
        in_specs=placed,
        out_specs=(
            P("dp", None, None),
            P("dp", None, None),
            P(None, "dp", "mp"),
            P(None, "dp", "mp"),
            P(None, "dp", "mp"),
            P("mp", "dp"),
            P("mp", "dp"),
            P("mp", "dp"),
            P("dp", "mp"),
            P("dp", "mp"),
            P("dp", "mp"),
            P("mp", "dp"),
            P("mp", "dp"),
            P("mp", "dp"),
            P(None, "mp", None),
            P(None, "mp", None),
            P(None, "mp", None),
            P("mp"),
            P("mp"),
            P("mp"),
            P(),
            P(),
            P(),
            P(),
            P(),
        ),
        check_vma=False,
    )
```

profile of v0, /device:TPU:0, one launch (start us, length us, event | category | flops | bytes accessed | tf_op | source)
XLA Modules:
  0.0 1091.9 jit_solution(17115793789987397871)
XLA Ops:
  33.1 6.5 fusion.61
  39.7 6.6 select_reduce_fusion
  46.4 6.6 select_reduce_fusion.1
  53.0 7.8 fusion.3
  60.9 6.6 fusion.97
  67.5 7.8 fusion.2
  81.7 6.7 select_reduce_fusion.2
  88.4 7.8 fusion.1
  96.1 6.6 fusion.95
  102.8 6.8 select_reduce_fusion.3
  109.6 7.8 fusion
  128.6 122.4 %all-reduce.8.cloned.1.call-done = f32[2048,768]{1,0:T(8,128)} async-done(((f32[2048,768]{1,0:T(8,128)}), f32[2048,768]{1,0:T(8,128)}) %all-reduce.8.cloned.1.call-update) | async-done | bytes 6291472 | tf_op jit(solution)/shard_map/psum | solution.py:116
  258.5 17.7 %multiply_convert_fusion.4 = (bf16[2048,768]{1,0:T(8,128)(2,1)}, f32[2048,768]{1,0:T(8,128)}, f32[2048,768]{1,0:T(8,128)}) fusion(f32[768]{0:T(1024)S(1)} %copy-done.103, bf16[2048,768]{1,0:T(8,128)(2,1)S(1)} %add_convert_fusion.2, f32[768,768]{1,0:T(8,128)S(1)} %copy-done.84), kind=kOutput, calls=%fused_computation.76 | convolution fusion | flops 2520317952 | bytes 21236736 | tf_op jit(solution)/shard_map/dot_general | solution.py:122
  276.2 8.2 convert_reduce_fusion.3
  293.8 8.1 fusion.101
  301.8 108.6 %all-reduce.10.cloned.1.call-done = f32[2048,768]{1,0:T(8,128)} async-done(((f32[2048,768]{1,0:T(8,128)}), f32[2048,768]{1,0:T(8,128)}) %all-reduce.10.cloned.1.call-update) | async-done | bytes 6291472 | tf_op jit(solution)/shard_map/psum | solution.py:142
  410.5 6.8 multiply_reduce_fusion.4
  426.7 6.8 multiply_reduce_fusion.3
  433.6 10.1 multiply_convert_fusion.3
  456.4 9.1 multiply_reduce_fusion.2
  471.3 7.4 multiply_reduce_fusion.1
  478.7 10.3 fusion.76
  489.0 9.2 multiply_reduce_fusion
  504.1 9.6 multiply_convert_fusion
  519.3 10.3 multiply_convert_fusion.2
  557.9 7.1 fusion.168
  595.2 183.8 %all-reduce.14.cloned.1.call-done = (f32[2048,768]{1,0:T(8,128)}, f32[2048,768]{1,0:T(8,128)}) async-done(((f32[2048,768]{1,0:T(8,128)}, f32[2048,768]{1,0:T(8,128)}), (f32[2048,768]{1,0:T(8,128)}, f32[2048,768]{1,0:T(8,128)})) %all-reduce.14.cloned.1.call-update) | async-done | bytes 12582928 | tf_op jit(solution)/shard_map/psum | solution.py:127
  779.0 16.2 %fusion.24 = (f32[768]{0:T(1024)S(1)}, f32[2048]{0:T(1024)S(1)}, f32[2048]{0:T(1024)S(1)}, f32[768]{0:T(1024)S(1)}, bf16[1,2048,768]{2,1,0:T(8,128)(2,1)}, /*index=5*/f32[]{:T(128)}, f32[768]{0:T(1024)S(1)}, f32[]{:T(128)}) fusion(f32[2048,768]{1,0:T(8,128)} %get-tuple-element.83, bf16[1,2048,768]{2,1,0:T(8,128)(2,1)S(1)} %copy-done.6, ...), kind=kLoop, calls=%fused_computation.53 | loop fusion | flops 39315200 | bytes 34662408 | tf_op jit(solution)/shard_map/reduce_sum | solution.py:193
  795.3 41.8 %all-reduce = (f32[]{:T(128)}, f32[5,3,64]{2,1,0:T(4,128)S(1)}, f32[768]{0:T(1024)S(1)}, f32[6,768]{1,0:T(8,128)S(1)}, f32[1]{0:T(128)}, /*index=5*/f32[1]{0:T(128)}) all-reduce(f32[]{:T(128)} %convert_reduce_fusion.5, f32[5,3,64]{2,1,0:T(4,128)S(1)} %pad_maximum_fusion.3, ...), channel_id=1, replica_groups=mesh['dp'=8,'mp'=4] {'dp'}, use_global_device_ids=true, to_apply=%region_33.34 | all-reduce | flops 6339 | bytes 50712 | tf_op jit(solution)/shard_map/psum | solution.py:133
  842.2 7.1 fusion.71
  849.4 171.1 %all-reduce.12.cloned.1.call-done = (f32[3,768,192]{1,2,0:T(8,128)}, f32[192,768]{1,0:T(8,128)}, f32[768,768]{1,0:T(8,128)}, f32[768,768]{0,1:T(8,128)}) async-done(((f32[3,768,192]{1,2,0:T(8,128)}, f32[192,768]{1,0:T(8,128)}, f32[768,768]{1,0:T(8,128)}, f32[768,768]{0,1:T(8,128)}), (f32[3,768,192]{1,2,0:T(8,128)}, f32[192,768]{1,0:T(8,128)}, f32[768,768]{1,0:T(8,128)}, ...) | async-done | bytes 7077904 | tf_op jit(solution)/shard_map/psum | solution.py:204
  1031.7 39.1 %psum.117 = f32[]{:T(128)} all-reduce(f32[]{:T(128)S(6)} %add.375), channel_id=1, replica_groups=mesh['dp'=8,'mp'=4] {'dp','mp'}, use_global_device_ids=true, to_apply=%region_58.59 | all-reduce | flops 1 | bytes 8 | tf_op jit(solution)/shard_map/psum | solution.py:225
  (386 shorter events, 179.6 us)
Async XLA Ops:
  7.2 243.7 %all-reduce.8.cloned.1.call-start = ((), (), s32[]{:S(2)}) async-start(), calls=%async_computation | async-start | bytes 12582912 | tf_op jit(solution)/shard_map/psum | solution.py:116
  9.5 21.7 %copy-start.70 = (f32[3,64]{1,0:T(4,128)}, f32[3,64]{1,0:T(4,128)S(1)}, u32[]{:S(2)}) copy-start(f32[3,64]{1,0:T(4,128)S(1)} %get-tuple-element.122) | copy-start | bytes 2308
  15.7 235.2 %copy-start.85 = (f32[768]{0:T(1024)}, f32[768]{0:T(1024)S(1)}, u32[]{:S(2)}) copy-start(f32[768]{0:T(1024)S(1)} %get-tuple-element.66) | copy-start | bytes 9220
  31.1 71.7 %copy-start.29 = (bf16[2048,3,64]{0,2,1:T(8,128)(2,1)}, bf16[2048,3,64]{0,2,1:T(8,128)(2,1)S(1)}, u32[]{:S(2)}) copy-start(bf16[2048,3,64]{0,2,1:T(8,128)(2,1)S(1)} %multiply_convert_fusion.7) | copy-start | bytes 2359300
  33.1 69.7 %copy-start.2 = (bf16[2048,3,64]{0,2,1:T(8,128)(2,1)}, bf16[2048,3,64]{0,2,1:T(8,128)(2,1)S(1)}, u32[]{:S(2)}) copy-start(bf16[2048,3,64]{0,2,1:T(8,128)(2,1)S(1)} %multiply_convert_fusion.6) | copy-start | bytes 2359300
  39.7 21.2 %copy-start.13 = (pred[512,2048]{1,0:T(8,128)(4,1)}, pred[512,2048]{1,0:T(8,128)(4,1)S(1)}, u32[]{:S(2)}) copy-start(pred[512,2048]{1,0:T(8,128)(4,1)S(1)} %get-tuple-element.126) | copy-start | bytes 3145732
  39.7 35.6 %copy-start.7 = (pred[512,2048]{1,0:T(8,128)(4,1)}, pred[512,2048]{1,0:T(8,128)(4,1)S(1)}, u32[]{:S(2)}) copy-start(pred[512,2048]{1,0:T(8,128)(4,1)S(1)} %get-tuple-element.125) | copy-start | bytes 3145732
  39.7 56.5 %copy-start.10 = (pred[512,2048]{1,0:T(8,128)(4,1)}, pred[512,2048]{1,0:T(8,128)(4,1)S(1)}, u32[]{:S(2)}) copy-start(pred[512,2048]{1,0:T(8,128)(4,1)S(1)} %get-tuple-element.124) | copy-start | bytes 3145732
  39.7 77.7 %copy-start.15 = (pred[512,2048]{1,0:T(8,128)(4,1)}, pred[512,2048]{1,0:T(8,128)(4,1)S(1)}, u32[]{:S(2)}) copy-start(pred[512,2048]{1,0:T(8,128)(4,1)S(1)} %get-tuple-element.123) | copy-start | bytes 3145732
  128.5 282.0 %all-reduce.10.cloned.1.call-start = ((), (), s32[]{:S(2)}) async-start(), calls=%async_computation.1 | async-start | bytes 12582912 | tf_op jit(solution)/shard_map/psum | solution.py:142
  128.6 288.7 %copy-start.74 = (f32[1,2048]{1,0:T(1,128)}, f32[1,2048]{1,0:T(1,128)S(1)}, u32[]{:S(2)}) copy-start(f32[1,2048]{1,0:T(1,128)S(1)} %convert_element_type.148) | copy-start | bytes 24580
  290.5 488.4 %all-reduce.14.cloned.1.call-start = ((), (), s32[]{:S(2)}) async-start(), calls=%async_computation.3 | async-start | bytes 25165824 | tf_op jit(solution)/shard_map/psum | solution.py:127
  293.8 139.8 %copy-start.61 = (f32[3,512]{1,0:T(4,128)}, f32[3,512]{1,0:T(4,128)S(1)}, u32[]{:S(2)}) copy-start(f32[3,512]{1,0:T(4,128)S(1)} %log_add_fusion.3) | copy-start | bytes 18436
  426.7 25.3 %slice-start.6 = ((s8[12582912]{0:T(1024)(128)(4,1)}), s8[4194304]{0:T(1024)(128)(4,1)S(1)}, s32[]{:S(2)}) async-start(s8[12582912]{0:T(1024)(128)(4,1)} %bitcast.194), calls=%async_computation.10 | async-start | bytes 8388608
  426.7 25.3 %slice-start.7 = ((s8[12582912]{0:T(1024)(128)(4,1)}), s8[4194304]{0:T(1024)(128)(4,1)S(1)}, s32[]{:S(2)}) async-start(s8[12582912]{0:T(1024)(128)(4,1)} %bitcast.194), calls=%async_computation.11 | async-start | bytes 8388608
  557.6 462.9 %all-reduce.12.cloned.1.call-start = ((), (), s32[]{:S(2)}) async-start(), calls=%async_computation.2 | async-start | bytes 14155776 | tf_op jit(solution)/shard_map/psum | solution.py:204
  779.0 63.2 %copy-start.83 = (f32[768]{0:T(1024)S(1)}, f32[768]{0:T(1024)}, u32[]{:S(2)}) copy-start(f32[768]{0:T(1024)} %copy-done.81) | copy-start | bytes 9220
  842.2 229.4 %copy-start.52 = (f32[3,96,192]{1,2,0:T(8,128)S(1)}, f32[3,96,192]{1,2,0:T(8,128)}, u32[]{:S(2)}) copy-start(f32[3,96,192]{1,2,0:T(8,128)} %copy.51) | copy-start | bytes 663556
  849.3 228.9 %copy-start.66 = (f32[192,96]{1,0:T(8,128)S(1)}, f32[192,96]{1,0:T(8,128)}, u32[]{:S(2)}) copy-start(f32[192,96]{1,0:T(8,128)} %param.36) | copy-start | bytes 221188
  849.3 228.9 %copy-start.67 = (f32[192,96]{1,0:T(8,128)S(1)}, f32[192,96]{1,0:T(8,128)}, u32[]{:S(2)}) copy-start(f32[192,96]{1,0:T(8,128)} %param.35) | copy-start | bytes 221188
  849.3 230.7 %copy-start.104 = (f32[768]{0:T(1024)S(1)}, f32[768]{0:T(1024)}, u32[]{:S(2)}) copy-start(f32[768]{0:T(1024)} %param.46) | copy-start | bytes 9220
  849.3 230.7 %copy-start.105 = (f32[768]{0:T(1024)S(1)}, f32[768]{0:T(1024)}, u32[]{:S(2)}) copy-start(f32[768]{0:T(1024)} %param.48) | copy-start | bytes 9220
  849.3 230.7 %copy-start.106 = (f32[768]{0:T(1024)S(1)}, f32[768]{0:T(1024)}, u32[]{:S(2)}) copy-start(f32[768]{0:T(1024)} %param.47) | copy-start | bytes 9220
  849.3 231.3 %copy-start.80 = (f32[5,3,64]{2,1,0:T(4,128)S(1)}, f32[5,3,64]{2,1,0:T(4,128)}, u32[]{:S(2)}) copy-start(f32[5,3,64]{2,1,0:T(4,128)} %param.43) | copy-start | bytes 11524
  849.3 231.3 %copy-start.97 = (f32[5,3,64]{2,1,0:T(4,128)S(1)}, f32[5,3,64]{2,1,0:T(4,128)}, u32[]{:S(2)}) copy-start(f32[5,3,64]{2,1,0:T(4,128)} %param.45) | copy-start | bytes 11524
  849.3 231.3 %copy-start.98 = (f32[5,3,64]{2,1,0:T(4,128)S(1)}, f32[5,3,64]{2,1,0:T(4,128)}, u32[]{:S(2)}) copy-start(f32[5,3,64]{2,1,0:T(4,128)} %param.44) | copy-start | bytes 11524
  849.3 231.9 %copy-start.69 = (f32[6,768]{1,0:T(8,128)S(1)}, f32[6,768]{1,0:T(8,128)}, u32[]{:S(2)}) copy-start(f32[6,768]{1,0:T(8,128)} %param.49) | copy-start | bytes 55300
  849.3 231.9 %copy-start.92 = (f32[6,768]{1,0:T(8,128)S(1)}, f32[6,768]{1,0:T(8,128)}, u32[]{:S(2)}) copy-start(f32[6,768]{1,0:T(8,128)} %param.51) | copy-start | bytes 55300
  849.4 231.9 %copy-start.93 = (f32[6,768]{1,0:T(8,128)S(1)}, f32[6,768]{1,0:T(8,128)}, u32[]{:S(2)}) copy-start(f32[6,768]{1,0:T(8,128)} %param.50) | copy-start | bytes 55300
  849.4 232.5 %copy-start.53 = (f32[768,96]{0,1:T(8,128)S(1)}, f32[768,96]{0,1:T(8,128)}, u32[]{:S(2)}) copy-start(f32[768,96]{0,1:T(8,128)} %copy.57) | copy-start | bytes 884740
  849.4 232.5 %copy-start.62 = (f32[768,96]{0,1:T(8,128)S(1)}, f32[768,96]{0,1:T(8,128)}, u32[]{:S(2)}) copy-start(f32[768,96]{0,1:T(8,128)} %param.42) | copy-start | bytes 884740
  849.4 232.5 %copy-start.63 = (f32[768,96]{0,1:T(8,128)S(1)}, f32[768,96]{0,1:T(8,128)}, u32[]{:S(2)}) copy-start(f32[768,96]{0,1:T(8,128)} %param.41) | copy-start | bytes 884740
  (102 other events, 705.2 us)
Sparse Core Ops, SparseCore 0:
  128.6 122.2 all-reduce.7
  290.7 119.7 all-reduce.9
  557.7 221.2 all-reduce.13
  783.2 237.2 all-reduce.11
where the time goes:
time: 1100 us; the launch traced here: 1090 us
  waiting for transfers between devices  586 us (53%)
  matrix products  205 us (19%)
  other arithmetic  164 us (15%)
  blocking collectives  80.9 us (7%)
  local copies, waits for them, and re-layouts  31.8 us (3%)
  between operations  24.1 us (2%)
    psum x1, waiting for transfers between devices, local(): lax.psum(jnp.dot(gated, down_low, preferred_element_type=jnp.float32), 'mp')  184 us
    psum x1, waiting for transfers between devices, local(): summed = lax.psum((grad_qkv, grad_outw, grad_up, grad_down), 'dp')  171 us
    psum x1, waiting for transfers between devices, local(): lax.psum(jnp.dot(mixed, out_low, preferred_element_type=jnp.float32), 'mp')  122 us
    psum x1, waiting for transfers between devices, local(): lax.psum(jnp.einsum('sf,df->sd', grad_upper, up_low, preferred_element_ty...  109 us
    psum x1, blocking collectives, local(): count, attn_total, mlp_total = lax.psum((count_here, attn_sq, mlp_sq), 'dp')  41.8 us
    psum x1, blocking collectives, local(): sq_total = lax.psum(raw_sq, ('dp', 'mp'))  39.1 us
    convert_element_type x4, other arithmetic, local(): grad_scores = (probs_full * (grad_probs - delta)).astype(jnp.bfloat16)  33.6 us
    dot_general x4, matrix products, local(): jnp.einsum('qhd,khd->hqk', grad_block, v_in, preferred_element_type=jnp.f...  32.5 us
  transfers between devices with their start and end apart: 4, of which 4 were waited for; matrix products, arithmetic and copies ran while one was open for 7% of the time, Pallas kernels for 0%

commit v1 on v0

--- a/solution.py
+++ b/solution.py
@@ -222,7 +222,8 @@
     raw_sq = (
         big_sq + jnp.where(first_dp, split_sq, 0.0) + jnp.where(first_dp & first_mp, whole_sq, 0.0)
     )
-    sq_total = lax.psum(raw_sq, ("dp", "mp"))
+    partial = lax.psum(raw_sq, "mp")
+    sq_total = lax.psum(partial, "dp")
     scale = seq_len * lax.axis_size("dp") / count
     grad_norm = scale * jnp.sqrt(sq_total)
     factor = jnp.minimum(1.0, CLIP_LIMIT / (grad_norm + 1e-06)) * scale

time: 1100 us -> 1100 us (level)
  blocking collectives: 80.9 us -> 68.6 us
  waiting for transfers between devices: 586 us -> 598 us
    psum x1, blocking collectives: 41.8 us -> 20 us  [local(): count, attn_total, mlp_total = lax.psum((count_here, attn_sq, mlp_sq), 'dp')]
    psum x1, waiting for transfers between devices: 171 us -> 184 us  [local(): summed = lax.psum((grad_qkv, grad_outw, grad_up, grad_down), 'dp')]
    psum x1 -> x2, blocking collectives: 39.1 us -> 48.6 us  [the longest x1 41.2 us: local(): lax.psum((vec_grad, head_grad, grad_bup), 'dp')]
  transfers between devices with their start and end apart: 4 -> 4, of which waited for: 4 -> 4; matrix products, arithmetic and copies ran while one was open for 7% -> 6% of each run, Pallas kernels for 0% -> 0%
where the time goes in v1:
time: 1100 us; the launch traced here: 1090 us
  waiting for transfers between devices  598 us (54%)
  matrix products  205 us (19%)
  other arithmetic  162 us (15%)
  blocking collectives  68.6 us (6%)
  local copies, waits for them, and re-layouts  34.7 us (3%)
  between operations  24.1 us (2%)
    psum x1, waiting for transfers between devices, local(): summed = lax.psum((grad_qkv, grad_outw, grad_up, grad_down), 'dp')  184 us
    psum x1, waiting for transfers between devices, local(): lax.psum(jnp.dot(gated, down_low, preferred_element_type=jnp.float32), 'mp')  184 us
    psum x1, waiting for transfers between devices, local(): lax.psum(jnp.dot(mixed, out_low, preferred_element_type=jnp.float32), 'mp')  122 us
    psum x1, waiting for transfers between devices, local(): lax.psum(jnp.einsum('sf,df->sd', grad_upper, up_low, preferred_element_ty...  109 us
    psum x1, blocking collectives, local(): lax.psum((vec_grad, head_grad, grad_bup), 'dp')  41.2 us
    convert_element_type x4, other arithmetic, local(): grad_scores = (probs_full * (grad_probs - delta)).astype(jnp.bfloat16)  33.6 us
    dot_general x4, matrix products, local(): jnp.einsum('qhd,khd->hqk', grad_block, v_in, preferred_element_type=jnp.f...  32.5 us
    reduce_sum x4, other arithmetic, local(): total = jnp.sum(expo, axis=-1, keepdims=True)  31.1 us
  transfers between devices with their start and end apart: 4, of which 4 were waited for; matrix products, arithmetic and copies ran while one was open for 6% of the time, Pallas kernels for 0%

profile of v1, /device:TPU:0, one launch (start us, length us, event | category | flops | bytes accessed | tf_op | source)
XLA Modules:
  0.0 1093.1 jit_solution(7242703862191913716)
XLA Ops:
  39.7 6.6 select_reduce_fusion
  46.4 6.6 select_reduce_fusion.1
  53.0 7.8 fusion.3
  60.9 6.6 fusion.97
  67.5 7.8 fusion.2
  81.7 6.7 select_reduce_fusion.2
  88.4 7.8 fusion.1
  96.2 6.6 fusion.95
  102.9 6.8 select_reduce_fusion.3
  109.6 7.8 fusion
  128.6 122.4 %all-reduce.9.cloned.1.call-done = f32[2048,768]{1,0:T(8,128)} async-done(((f32[2048,768]{1,0:T(8,128)}), f32[2048,768]{1,0:T(8,128)}) %all-reduce.9.cloned.1.call-update) | async-done | bytes 6291472 | tf_op jit(solution)/shard_map/psum | solution.py:116
  258.5 17.7 %multiply_convert_fusion.4 = (bf16[2048,768]{1,0:T(8,128)(2,1)}, f32[2048,768]{1,0:T(8,128)}, f32[2048,768]{1,0:T(8,128)}) fusion(f32[768]{0:T(1024)S(1)} %copy-done.101, bf16[2048,768]{1,0:T(8,128)(2,1)S(1)} %add_convert_fusion.2, f32[768,768]{1,0:T(8,128)S(1)} %copy-done.81), kind=kOutput, calls=%fused_computation.76 | convolution fusion | flops 2520317952 | bytes 21236736 | tf_op jit(solution)/shard_map/dot_general | solution.py:122
  276.2 8.2 convert_reduce_fusion.3
  293.8 8.1 fusion.101
  301.9 108.6 %all-reduce.11.cloned.1.call-done = f32[2048,768]{1,0:T(8,128)} async-done(((f32[2048,768]{1,0:T(8,128)}), f32[2048,768]{1,0:T(8,128)}) %all-reduce.11.cloned.1.call-update) | async-done | bytes 6291472 | tf_op jit(solution)/shard_map/psum | solution.py:142
  410.5 6.8 multiply_reduce_fusion.4
  426.7 6.8 multiply_reduce_fusion.3
  433.6 10.1 multiply_convert_fusion.3
  456.4 9.1 multiply_reduce_fusion.2
  471.3 7.4 multiply_reduce_fusion.1
  478.7 10.3 fusion.76
  489.0 9.2 multiply_reduce_fusion
  504.1 9.5 multiply_convert_fusion
  519.3 10.3 multiply_convert_fusion.2
  557.9 7.1 fusion.168
  595.3 183.7 %all-reduce.15.cloned.1.call-done = (f32[2048,768]{1,0:T(8,128)}, f32[2048,768]{1,0:T(8,128)}) async-done(((f32[2048,768]{1,0:T(8,128)}, f32[2048,768]{1,0:T(8,128)}), (f32[2048,768]{1,0:T(8,128)}, f32[2048,768]{1,0:T(8,128)})) %all-reduce.15.cloned.1.call-update) | async-done | bytes 12582928 | tf_op jit(solution)/shard_map/psum | solution.py:127
  779.0 13.3 %fusion.24 = (f32[768]{0:T(1024)S(1)}, f32[2048]{0:T(1024)S(1)}, f32[2048]{0:T(1024)S(1)}, f32[768]{0:T(1024)S(1)}, bf16[1,2048,768]{2,1,0:T(8,128)(2,1)}, /*index=5*/f32[]{:T(128)}, f32[768]{0:T(1024)S(1)}, f32[]{:T(128)}) fusion(f32[2048,768]{1,0:T(8,128)} %get-tuple-element.84, bf16[1,2048,768]{2,1,0:T(8,128)(2,1)S(1)} %copy-done.6, ...), kind=kLoop, calls=%fused_computation.53 | loop fusion | flops 39315200 | bytes 34662408 | tf_op jit(solution)/shard_map/reduce_sum | solution.py:193
  792.4 41.2 %all-reduce.1 = (f32[5,3,64]{2,1,0:T(4,128)S(1)}, f32[768]{0:T(1024)S(1)}, f32[6,768]{1,0:T(8,128)S(1)}) all-reduce(f32[5,3,64]{2,1,0:T(4,128)S(1)} %pad_maximum_fusion.3, f32[768]{0:T(1024)} %get-tuple-element.150, f32[6,768]{1,0:T(8,128)S(1)} %stack.49), channel_id=1, replica_groups=mesh['dp'=8,'mp'=4] {'dp'}, use_global_device_ids=true, to_apply=%region_45.46 | all-reduce | flops 6336 | bytes 50688 | tf_op jit(solution)/shard_map/psum | solution.py:200
  837.4 183.7 %all-reduce.13.cloned.1.call-done = (f32[3,768,192]{1,2,0:T(8,128)}, f32[192,768]{1,0:T(8,128)}, f32[768,768]{1,0:T(8,128)}, f32[768,768]{0,1:T(8,128)}) async-done(((f32[3,768,192]{1,2,0:T(8,128)}, f32[192,768]{1,0:T(8,128)}, f32[768,768]{1,0:T(8,128)}, f32[768,768]{0,1:T(8,128)}), (f32[3,768,192]{1,2,0:T(8,128)}, f32[192,768]{1,0:T(8,128)}, f32[768,768]{1,0:T(8,128)}, ...) | async-done | bytes 7077904 | tf_op jit(solution)/shard_map/psum | solution.py:204
  1030.5 7.4 psum.124
  1037.9 20.0 %all-reduce = (f32[]{:T(128)}, f32[]{:T(128)}, f32[1]{0:T(128)}, f32[1]{0:T(128)}) all-reduce(f32[]{:T(128)} %convert_reduce_fusion.5, f32[]{:T(128)} %psum.124, f32[1]{0:T(128)} %bitcast.52, f32[1]{0:T(128)} %bitcast.51), channel_id=1, replica_groups=mesh['dp'=8,'mp'=4] {'dp'}, use_global_device_ids=true, to_apply=%region_33.34 | all-reduce | flops 4 | bytes 32 | tf_op jit(solution)/shard_map/psum | solution.py:133
  1072.3 7.0 fusion.71
  (383 shorter events, 190.1 us)
Async XLA Ops:
  7.2 243.7 %all-reduce.9.cloned.1.call-start = ((), (), s32[]{:S(2)}) async-start(), calls=%async_computation | async-start | bytes 12582912 | tf_op jit(solution)/shard_map/psum | solution.py:116
  9.5 21.7 %copy-start.68 = (f32[3,64]{1,0:T(4,128)}, f32[3,64]{1,0:T(4,128)S(1)}, u32[]{:S(2)}) copy-start(f32[3,64]{1,0:T(4,128)S(1)} %get-tuple-element.123) | copy-start | bytes 2308
  15.7 235.3 %copy-start.82 = (f32[768]{0:T(1024)}, f32[768]{0:T(1024)S(1)}, u32[]{:S(2)}) copy-start(f32[768]{0:T(1024)S(1)} %get-tuple-element.66) | copy-start | bytes 9220
  24.5 15.2 %copy-start.56 = (f32[2048,3]{0,1:T(4,128)}, f32[2048,3]{0,1:T(4,128)S(1)}, u32[]{:S(2)}) copy-start(f32[2048,3]{0,1:T(4,128)S(1)} %broadcast_multiply_fusion.5) | copy-start | bytes 73732
  26.2 20.2 %copy-start.58 = (f32[2048,3]{0,1:T(4,128)}, f32[2048,3]{0,1:T(4,128)S(1)}, u32[]{:S(2)}) copy-start(f32[2048,3]{0,1:T(4,128)S(1)} %add_rsqrt_fusion.1) | copy-start | bytes 73732
  27.8 18.6 %copy-start.48 = (f32[2048,3]{0,1:T(4,128)}, f32[2048,3]{0,1:T(4,128)S(1)}, u32[]{:S(2)}) copy-start(f32[2048,3]{0,1:T(4,128)S(1)} %broadcast_multiply_fusion.4) | copy-start | bytes 73732
  29.4 16.9 %copy-start.50 = (f32[2048,3]{0,1:T(4,128)}, f32[2048,3]{0,1:T(4,128)S(1)}, u32[]{:S(2)}) copy-start(f32[2048,3]{0,1:T(4,128)S(1)} %add_rsqrt_fusion) | copy-start | bytes 73732
  31.2 71.7 %copy-start.29 = (bf16[2048,3,64]{0,2,1:T(8,128)(2,1)}, bf16[2048,3,64]{0,2,1:T(8,128)(2,1)S(1)}, u32[]{:S(2)}) copy-start(bf16[2048,3,64]{0,2,1:T(8,128)(2,1)S(1)} %multiply_convert_fusion.7) | copy-start | bytes 2359300
  33.1 69.7 %copy-start.2 = (bf16[2048,3,64]{0,2,1:T(8,128)(2,1)}, bf16[2048,3,64]{0,2,1:T(8,128)(2,1)S(1)}, u32[]{:S(2)}) copy-start(bf16[2048,3,64]{0,2,1:T(8,128)(2,1)S(1)} %multiply_convert_fusion.6) | copy-start | bytes 2359300
  39.7 21.2 %copy-start.13 = (pred[512,2048]{1,0:T(8,128)(4,1)}, pred[512,2048]{1,0:T(8,128)(4,1)S(1)}, u32[]{:S(2)}) copy-start(pred[512,2048]{1,0:T(8,128)(4,1)S(1)} %get-tuple-element.127) | copy-start | bytes 3145732
  39.7 35.6 %copy-start.7 = (pred[512,2048]{1,0:T(8,128)(4,1)}, pred[512,2048]{1,0:T(8,128)(4,1)S(1)}, u32[]{:S(2)}) copy-start(pred[512,2048]{1,0:T(8,128)(4,1)S(1)} %get-tuple-element.126) | copy-start | bytes 3145732
  39.7 56.5 %copy-start.10 = (pred[512,2048]{1,0:T(8,128)(4,1)}, pred[512,2048]{1,0:T(8,128)(4,1)S(1)}, u32[]{:S(2)}) copy-start(pred[512,2048]{1,0:T(8,128)(4,1)S(1)} %get-tuple-element.125) | copy-start | bytes 3145732
  39.7 77.7 %copy-start.15 = (pred[512,2048]{1,0:T(8,128)(4,1)}, pred[512,2048]{1,0:T(8,128)(4,1)S(1)}, u32[]{:S(2)}) copy-start(pred[512,2048]{1,0:T(8,128)(4,1)S(1)} %get-tuple-element.124) | copy-start | bytes 3145732
  46.4 14.5 %copy-start.75 = (f32[3,512]{1,0:T(4,128)}, f32[3,512]{1,0:T(4,128)S(1)}, u32[]{:S(2)}) copy-start(f32[3,512]{1,0:T(4,128)S(1)} %get-tuple-element.132) | copy-start | bytes 18436
  128.5 282.0 %all-reduce.11.cloned.1.call-start = ((), (), s32[]{:S(2)}) async-start(), calls=%async_computation.1 | async-start | bytes 12582912 | tf_op jit(solution)/shard_map/psum | solution.py:142
  128.6 288.7 %copy-start.72 = (f32[1,2048]{1,0:T(1,128)}, f32[1,2048]{1,0:T(1,128)S(1)}, u32[]{:S(2)}) copy-start(f32[1,2048]{1,0:T(1,128)S(1)} %convert_element_type.148) | copy-start | bytes 24580
  258.5 17.7 %copy-start.41 = (bf16[2048,768]{1,0:T(8,128)(2,1)}, bf16[2048,768]{1,0:T(8,128)(2,1)S(1)}, u32[]{:S(2)}) copy-start(bf16[2048,768]{1,0:T(8,128)(2,1)S(1)} %add_convert_fusion.2) | copy-start | bytes 9437188
  258.5 17.7 %copy-start.25 = (bf16[1,2048,768]{2,1,0:T(8,128)(2,1)S(1)}, bf16[1,2048,768]{2,1,0:T(8,128)(2,1)}, u32[]{:S(2)}) copy-start(bf16[1,2048,768]{2,1,0:T(8,128)(2,1)} %param.27) | copy-start | bytes 9437188
  258.5 17.7 %copy-start.77 = (f32[768,768]{1,0:T(8,128)S(1)}, f32[768,768]{1,0:T(8,128)}, u32[]{:S(2)}) copy-start(f32[768,768]{1,0:T(8,128)} %param.40) | copy-start | bytes 7077892
  290.6 488.4 %all-reduce.15.cloned.1.call-start = ((), (), s32[]{:S(2)}) async-start(), calls=%async_computation.3 | async-start | bytes 25165824 | tf_op jit(solution)/shard_map/psum | solution.py:127
  293.8 139.8 %copy-start.61 = (f32[3,512]{1,0:T(4,128)}, f32[3,512]{1,0:T(4,128)S(1)}, u32[]{:S(2)}) copy-start(f32[3,512]{1,0:T(4,128)S(1)} %log_add_fusion.3) | copy-start | bytes 18436
  426.7 25.3 %slice-start.6 = ((s8[12582912]{0:T(1024)(128)(4,1)}), s8[4194304]{0:T(1024)(128)(4,1)S(1)}, s32[]{:S(2)}) async-start(s8[12582912]{0:T(1024)(128)(4,1)} %bitcast.194), calls=%async_computation.10 | async-start | bytes 8388608
  426.7 25.3 %slice-start.7 = ((s8[12582912]{0:T(1024)(128)(4,1)}), s8[4194304]{0:T(1024)(128)(4,1)S(1)}, s32[]{:S(2)}) async-start(s8[12582912]{0:T(1024)(128)(4,1)} %bitcast.194), calls=%async_computation.11 | async-start | bytes 8388608
  433.6 18.5 %slice-start.8 = ((s8[12582912]{0:T(1024)(128)(4,1)}), s8[4194304]{0:T(1024)(128)(4,1)S(1)}, s32[]{:S(2)}) async-start(s8[12582912]{0:T(1024)(128)(4,1)} %bitcast.194), calls=%async_computation.12 | async-start | bytes 8388608
  452.1 13.4 %slice-start = ((s8[12582912]{0:T(1024)(128)(4,1)}), s8[4194304]{0:T(1024)(128)(4,1)S(1)}, s32[]{:S(2)}) async-start(s8[12582912]{0:T(1024)(128)(4,1)} %bitcast.190), calls=%async_computation.4 | async-start | bytes 8388608
  471.3 17.7 %slice-start.3 = ((s8[12582912]{0:T(1024)(128)(4,1)}), s8[4194304]{0:T(1024)(128)(4,1)S(1)}, s32[]{:S(2)}) async-start(s8[12582912]{0:T(1024)(128)(4,1)} %bitcast.192), calls=%async_computation.7 | async-start | bytes 8388608
  471.3 17.7 %slice-start.4 = ((s8[12582912]{0:T(1024)(128)(4,1)}), s8[4194304]{0:T(1024)(128)(4,1)S(1)}, s32[]{:S(2)}) async-start(s8[12582912]{0:T(1024)(128)(4,1)} %bitcast.192), calls=%async_computation.8 | async-start | bytes 8388608
  519.3 17.2 %slice-start.14 = ((s8[12582912]{0:T(1024)(128)(4,1)}), s8[4194304]{0:T(1024)(128)(4,1)S(1)}, s32[]{:S(2)}) async-start(s8[12582912]{0:T(1024)(128)(4,1)} %bitcast.200), calls=%async_computation.18 | async-start | bytes 8388608
  519.3 17.2 %slice-start.15 = ((s8[12582912]{0:T(1024)(128)(4,1)}), s8[4194304]{0:T(1024)(128)(4,1)S(1)}, s32[]{:S(2)}) async-start(s8[12582912]{0:T(1024)(128)(4,1)} %bitcast.200), calls=%async_computation.19 | async-start | bytes 8388608
  557.6 463.5 %all-reduce.13.cloned.1.call-start = ((), (), s32[]{:S(2)}) async-start(), calls=%async_computation.2 | async-start | bytes 14155776 | tf_op jit(solution)/shard_map/psum | solution.py:204
  779.0 280.9 %copy-start.52 = (f32[3,96,192]{1,2,0:T(8,128)S(1)}, f32[3,96,192]{1,2,0:T(8,128)}, u32[]{:S(2)}) copy-start(f32[3,96,192]{1,2,0:T(8,128)} %copy.51) | copy-start | bytes 663556
  833.6 236.5 %copy-start.91 = (f32[768]{0:T(1024)}, f32[768]{0:T(1024)S(1)}, u32[]{:S(2)}) copy-start(f32[768]{0:T(1024)S(1)} %get-tuple-element.77) | copy-start | bytes 9220
  (100 other events, 544.7 us)
Sparse Core Ops, SparseCore 0:
  128.7 122.2 all-reduce.8
  290.7 119.7 all-reduce.10
  557.7 221.2 all-reduce.14
  783.8 237.2 all-reduce.12
